TPU v7x, 512 devices: a whole 4x8x8 slice. The times are simulated.
512 devices in a mesh: gx: 16 (over x, z_hi), gy: 32 (over y, z_lo, core).
Axes of the slice: x: 4, y: 8, z: 8 (z_hi: 4, z_lo: 2; z = z_hi * 2 + z_lo), core: 2. Of those that a mesh axis runs over, the one named last changes fastest.
Arguments:
- object_field: float32 [2, 2, 8192, 4096], P(None, None, 'gy', 'gx'), may hold values from -5 to 5
- probe: float32 [2, 256, 256], replicated, may hold values from -6 to 6
- positions: int32 [64, 16, 2], P('gy', 'gx'), may hold values from 0 to 256, as said below
- residual: bfloat16 [64, 16, 2, 256, 256], P('gy', 'gx'), may hold values from -6 to 6
- saved_wave: bfloat16 [64, 16, 2, 256, 256], P('gy', 'gx'), may hold values from -6 to 6
Outputs:
- new_object: float32 [2, 2, 8192, 4096], P(None, None, 'gy', 'gx')
Inputs may be any that keep to these rules, and one draw needn't show every extreme that they name: `positions`: row and column of each position's window corner in a frame whose anchor lies 128 cells above and to the left of its tile's first cell, so that the window stays within 128 cells of the tile; position p of a tile lies near row 128 and column 128 * (1 + p mod 2) of that frame.
All inputs are finite; a program needn't handle non-finite values.
Results may differ from a plain program's by a relative error of at most 0.0003.
Values sent between devices are 32-bit elements; how exact they have to be, the bound alone decides.
A program may use at most 64 MiB of HBM per device.

v0:
```python
import math

import jax
import jax.numpy as jnp
from jax import lax
from jax.sharding import PartitionSpec as P

fresnel_rate = 200.0
ridge = 0.5


def padded(block, sides, width):
    for axis, dim in sides:
        count = lax.axis_size(axis)
        forward = [(i, i + 1) for i in range(count - 1)]
        backward = [(target, source) for source, target in forward]
        low = lax.ppermute(
            lax.slice_in_dim(block, block.shape[dim] - width, None, axis=dim), axis, forward
        )
        high = lax.ppermute(lax.slice_in_dim(block, 0, width, axis=dim), axis, backward)
        block = jnp.concatenate([low, block, high], axis=dim)
    return block


def from_behind(value, axis, steps):
    count = lax.axis_size(axis)
    leading, last = (max(0, -steps), min(count, count - steps))
    return lax.ppermute(value, axis, [(source, source + steps) for source in range(leading, last)])


def kernel_conj(size):
    index = jnp.arange(size, dtype=jnp.int32)
    freq = ((index + size // 2) % size - size // 2).astype(jnp.float32) / size
    phase = fresnel_rate * (freq[:, None] ** 2 + freq[None, :] ** 2)
    return (jnp.cos(phase), jnp.sin(phase))


def block_tables(size, inverse):
    index = jnp.arange(size, dtype=jnp.int32)
    product = index[:, None] * index[None, :] % size
    angle = product.astype(jnp.float32) * (2.0 * math.pi / size)
    scale = 1.0 / math.sqrt(size)
    table_re = jnp.cos(angle) * scale
    table_im = -jnp.sin(angle) * scale
    if inverse:
        table_im = -table_im
    left_table = jnp.stack([jnp.stack([table_re, -table_im]), jnp.stack([table_im, table_re])])
    right_table = jnp.stack([jnp.stack([table_re, table_im]), jnp.stack([-table_im, table_re])])
    return (left_table, right_table)


def transform(fields, inverse):
    left_table, right_table = block_tables(fields.shape[-1], inverse)
    inner = jnp.einsum("abjk,pbkl->pajl", left_table, fields, precision=lax.Precision.HIGHEST)
    return jnp.einsum("pbjk,bakl->pajl", inner, right_table, precision=lax.Precision.HIGHEST)


def shards(object_field, probe, positions, residual, saved_wave):
    window = probe.shape[-1]
    margin = window // 2
    spots = positions.reshape(-1, 2)
    spot_count = spots.shape[0]
    second = object_field[1]
    second_ext = padded(second, (("gx", 2), ("gy", 1)), margin)
    detector = residual.reshape(spot_count, 2, window, window).astype(jnp.float32)
    wave = saved_wave.reshape(spot_count, 2, window, window).astype(jnp.float32)
    anchor = jnp.zeros((), jnp.int32)
    patches = jnp.stack(
        [
            lax.dynamic_slice(
                second_ext, (anchor, spots[number, 0], spots[number, 1]), (2, window, window)
            )
            for number in range(spot_count)
        ]
    )
    field = transform(detector, True)
    field_re = field[:, 0]
    field_im = field[:, 1]
    patch_re = patches[:, 0]
    patch_im = patches[:, 1]
    chi = jnp.stack(
        [patch_re * field_re + patch_im * field_im, patch_re * field_im - patch_im * field_re],
        axis=1,
    )
    spec = transform(chi, False)
    kernel_re, kernel_im = kernel_conj(window)
    spec_re = spec[:, 0]
    spec_im = spec[:, 1]
    moved = jnp.stack(
        [kernel_re * spec_re - kernel_im * spec_im, kernel_re * spec_im + kernel_im * spec_re],
        axis=1,
    )
    back = transform(moved, True)
    back_re = back[:, 0]
    back_im = back[:, 1]
    probe_re = probe[0]
    probe_im = probe[1]
    first_re = probe_re * back_re + probe_im * back_im
    first_im = probe_re * back_im - probe_im * back_re
    wave_re = wave[:, 0]
    wave_im = wave[:, 1]
    second_re = wave_re * field_re + wave_im * field_im
    second_im = wave_re * field_im - wave_im * field_re
    light = probe_re * probe_re + probe_im * probe_im
    parts = [first_re, first_im, second_re, second_im]
    planes = jnp.stack(parts + [jnp.broadcast_to(light, first_re.shape)], axis=1)
    channels = planes.shape[1]
    summed = jnp.zeros((channels, 2 * window, 2 * window), jnp.float32)
    for number in range(spot_count):
        corner = (anchor, spots[number, 0], spots[number, 1])
        current = lax.dynamic_slice(summed, corner, (channels, window, window))
        summed = lax.dynamic_update_slice(summed, current + planes[number], corner)
    from_rows = []
    for direction in (1, -1):
        edge_rows = summed[:, 3 * margin :, :] if direction == 1 else summed[:, :margin, :]
        from_rows.append(from_behind(edge_rows, "gy", direction))
    row_total = summed[:, margin : 3 * margin, :] + jnp.concatenate(from_rows, axis=1)
    from_columns = []
    for direction in (1, -1):
        edge_columns = row_total[:, :, 3 * margin :] if direction == 1 else row_total[:, :, :margin]
        from_columns.append(from_behind(edge_columns, "gx", direction))
    total = row_total[:, :, margin : 3 * margin] + jnp.concatenate(from_columns, axis=2)
    light_tile = total[4]
    grads = total[:4].reshape(2, 2, window, window)
    return object_field - grads / (light_tile + ridge)


def solution(mesh):
    placed = (
        P(None, None, "gy", "gx"),
        P(),
        P("gy", "gx", None),
        P("gy", "gx", None, None, None),
        P("gy", "gx", None, None, None),
    )
    return jax.shard_map(
        shards, mesh=mesh, in_specs=placed, out_specs=P(None, None, "gy", "gx"), check_vma=False
    )
```

profile of v0, /device:TPU:37, one launch (start us, length us, event | category | flops | bytes accessed | tf_op | source)
XLA Modules:
  0.0 178.8 jit_solution(11105698561946192558)
XLA Ops:
  0.0 1.2 slice_bitcast_fusion.2
  1.2 5.8 %collective-permute-start = (f32[2,256,128]{2,1,0:T(8,128)S(1)}, f32[2,256,128]{2,1,0:T(8,128)S(1)}, u32[]{:S(2)}, u32[]{:S(2)}) collective-permute-start(f32[2,256,128]{2,1,0:T(8,128)S(1)} %get-tuple-element.19), channel_id=1, source_target_pairs={{0,32},{32,64},{64,96},{96,128},{128,160},{160,192},{192,224},{224... | collective-permute-start | bytes 786440 | tf_op jit(solution)/shard_map/ppermute | solution.py:17
  7.0 6.7 %collective-permute-start.1 = (f32[2,256,128]{2,1,0:T(8,128)S(1)}, f32[2,256,128]{2,1,0:T(8,128)S(1)}, u32[]{:S(2)}, u32[]{:S(2)}) collective-permute-start(f32[2,256,128]{2,1,0:T(8,128)S(1)} %get-tuple-element.20), channel_id=1, source_target_pairs={{32,0},{64,32},{96,64},{128,96},{160,128},{192,160},{224,192},{256... | collective-permute-start | bytes 786440 | tf_op jit(solution)/shard_map/ppermute | solution.py:20
  13.8 1.0 fusion.23
  14.8 1.1 negate_multiply_fusion
  15.9 0.1 fusion.11
  16.0 0.0 copy-start.2
  16.1 1.0 convolution_bitcast_fusion.5
  17.1 0.0 copy-start.18
  17.1 1.9 %convolution_bitcast_fusion.4 = f32[2,2,256,256]{2,3,0,1:T(8,128)S(1)} fusion(f32[2,2,256,256,1]{3,2,1,0,4:T(8,128)S(1)} %convolution_bitcast_fusion.5, f32[1,2,256,256]{2,3,0,1:T(8,128)S(1)} %get-tuple-element.22, f32[1,2,256,256]{2,3,0,1:T(8,128)S(1)} %get-tuple-element.25), kind=kOutput, calls=%fused_computation.6 | convolution fusion | flops 1610874880 | bytes 3145728 | tf_op jit(solution)/shard_map/pbjk,bakl->pajl/dot_general | solution.py:55
  19.0 0.7 fusion.35
  19.8 0.0 copy-start.17
  19.8 0.0 collective-permute-done
  19.8 5.1 %collective-permute-done.1 = f32[2,256,128]{2,1,0:T(8,128)S(1)} collective-permute-done((f32[2,256,128]{2,1,0:T(8,128)S(1)}, f32[2,256,128]{2,1,0:T(8,128)S(1)}, u32[]{:S(2)}, u32[]{:S(2)}) %collective-permute-start.1) | collective-permute-done | bytes 262176 | tf_op jit(solution)/shard_map/ppermute | solution.py:20
  24.9 0.1 pad_maximum_fusion.2
  25.0 1.1 fusion.33
  26.1 4.8 %collective-permute-start.2 = (f32[2,128,512]{2,1,0:T(8,128)}, f32[2,128,512]{2,1,0:T(8,128)}, u32[]{:S(2)}, u32[]{:S(2)}) collective-permute-start(f32[2,128,512]{2,1,0:T(8,128)} %get-tuple-element.15), channel_id=1, source_target_pairs={{0,1},{1,2},{2,3},{3,4},{4,5},{5,6},{6,7},{7,8},{8,9},{9,10},{10,1... | collective-permute-start | bytes 1572872 | tf_op jit(solution)/shard_map/ppermute | solution.py:17
  30.8 1.9 %collective-permute-start.3 = (f32[2,128,512]{2,1,0:T(8,128)}, f32[2,128,512]{2,1,0:T(8,128)}, u32[]{:S(2)}, u32[]{:S(2)}) collective-permute-start(f32[2,128,512]{2,1,0:T(8,128)} %get-tuple-element.16), channel_id=1, source_target_pairs={{1,0},{2,1},{3,2},{4,3},{5,4},{6,5},{7,6},{8,7},{9,8},{10,9},{11,1... | collective-permute-start | bytes 1572872 | tf_op jit(solution)/shard_map/ppermute | solution.py:20
  37.8 0.9 copy.13
  38.7 1.0 copy.12
  39.7 0.1 copy.6
  39.8 0.9 copy.11
  43.2 2.0 %fusion.19 = (f32[256,256]{0,1:T(8,128)}, f32[256,256]{0,1:T(8,128)}) fusion(f32[256]{0:T(256)S(1)} %fusion.27), kind=kLoop, calls=%fused_computation.61 | loop fusion | flops 131072 | bytes 525312 | tf_op jit(solution)/shard_map/cos | solution.py:35
  45.2 1.1 bitcast_convert_fusion
  46.4 0.0 collective-permute-done.3
  46.4 1.8 pad_maximum_fusion
  48.1 1.3 constant_dynamic-slice_fusion.1
  49.5 2.0 %copy.8 = f32[2,256,256]{1,2,0:T(8,128)} copy(f32[2,256,256]{2,1,0:T(8,128)} %get-tuple-element.11) | data formatting | bytes 1048576 | tf_op jit(solution)/shard_map/dynamic_slice | solution.py:70
  51.5 2.1 %copy.9 = f32[2,256,256]{1,2,0:T(8,128)} copy(f32[2,256,256]{2,1,0:T(8,128)} %get-tuple-element.12) | data formatting | bytes 1048576 | tf_op jit(solution)/shard_map/dynamic_slice | solution.py:70
  53.6 1.6 multiply_add_fusion.1
  55.2 0.0 copy-start.3
  55.2 0.0 copy-done.7
  55.3 1.9 %convolution_bitcast_fusion.3 = f32[2,2,256,256,1]{3,2,1,0,4:T(8,128)S(1)} fusion(f32[1,2,256,256]{2,3,0,1:T(8,128)S(1)} %copy-done.5, f32[1,2,256,256]{2,3,0,1:T(8,128)S(1)} %copy-done.7, f32[2,1,256,256]{2,3,0,1:T(8,128)S(1)} %get-tuple-element.10, f32[2,1,256,256]{2,3,0,1:T(8,128)S(1)} %get-tuple-element.9), kind=kOutput, calls=%fused_computation.5 | convolution fusion | flops 1611137024 | bytes 3145728 | tf_op jit(solution)/shard_map/abjk,pbkl->pajl/dot_general | solution.py:54
  57.2 1.9 %convolution_bitcast_fusion.2 = f32[2,2,256,256]{2,3,0,1:T(8,128)S(1)} fusion(f32[2,2,256,256,1]{3,2,1,0,4:T(8,128)S(1)} %convolution_bitcast_fusion.3, f32[1,2,256,256]{2,3,1,0:T(8,128)S(1)} %copy-done.3, f32[1,2,256,256]{2,3,1,0:T(8,128)S(1)} %get-tuple-element.21), kind=kOutput, calls=%fused_computation.4 | convolution fusion | flops 1610874880 | bytes 3145728 | tf_op jit(solution)/shard_map/pbjk,bakl->pajl/dot_general | solution.py:55
  59.1 0.1 multiply_subtract_fusion
  59.2 1.9 %convolution_bitcast_fusion.1 = f32[2,2,256,256,1]{3,2,1,0,4:T(8,128)S(1)} fusion(f32[1,2,256,256]{2,3,1,0:T(8,128)S(1)} %copy-done.3, f32[1,2,256,256]{2,3,1,0:T(8,128)S(1)} %get-tuple-element.21, f32[2,1,256,256]{2,3,0,1:T(8,128)S(1)} %get-tuple-element.14, f32[2,1,256,256]{2,3,0,1:T(8,128)S(1)} %get-tuple-element.13), kind=kOutput, calls=%fused_computation.3 | convolution fusion | flops 1611137024 | bytes 3145728 | tf_op jit(solution)/shard_map/abjk,pbkl->pajl/dot_general | solution.py:54
  61.1 1.9 %convolution_bitcast_fusion = f32[2,2,256,256]{2,3,0,1:T(8,128)S(1)} fusion(f32[2,2,256,256,1]{3,2,1,0,4:T(8,128)S(1)} %convolution_bitcast_fusion.1, f32[1,2,256,256]{2,3,0,1:T(8,128)S(1)} %copy-done.5, f32[1,2,256,256]{2,3,0,1:T(8,128)S(1)} %copy-done.7), kind=kOutput, calls=%fused_computation.2 | convolution fusion | flops 1610874880 | bytes 3145728 | tf_op jit(solution)/shard_map/pbjk,bakl->pajl/dot_general | solution.py:55
  63.0 0.1 add_dynamic-update-slice_fusion.1
  63.1 0.1 subtract_dynamic-update-slice_fusion.1
  63.2 0.1 add_dynamic-update-slice_fusion
  63.4 0.1 subtract_dynamic-update-slice_fusion
  63.5 0.7 copy-done.12
  64.2 1.5 copy-done.9
  65.7 0.1 slice_bitcast_fusion.1
  65.8 3.0 %broadcast_in_dim.2 = f32[5,512,512]{1,2,0:T(8,128)} broadcast(f32[]{:T(128)} %constant.39.clone.1), dimensions={} | broadcast | bytes 5242884 | tf_op jit(solution)/shard_map/broadcast_in_dim | solution.py:108
  68.8 14.5 %dynamic_update_slice.6 = f32[5,512,512]{1,2,0:T(8,128)} dynamic-update-slice(f32[5,512,512]{1,2,0:T(8,128)} %broadcast_in_dim.2, f32[5,256,256]{1,2,0:T(8,128)S(1)} %slice_bitcast_fusion.1, s32[]{:T(128)} %constant.40.clone.1, s32[]{:T(128)S(6)} %select_n.81, s32[]{:T(128)S(6)} %select_n.82) | dynamic-update-slice | bytes 2621444 | tf_op jit(solution)/shard_map/dynamic_update_slice | solution.py:112
  83.4 2.4 %fusion = f32[5,256,256]{1,2,0:T(8,128)S(1)} fusion(f32[2,5,256,256]{2,3,0,1:T(8,128)} %copy-done.9, f32[5,512,512]{1,2,0:T(8,128)} %dynamic_update_slice.6, s32[]{:T(128)S(6)} %select_n.83, s32[]{:T(128)S(6)} %select_n.84), kind=kLoop, calls=%fused_computation.10 | loop fusion | flops 327680 | bytes 3932168 | tf_op jit(solution)/shard_map/add | solution.py:112
  85.7 13.2 %dynamic_update_slice.7 = f32[5,512,512]{1,2,0:T(8,128)} dynamic-update-slice(f32[5,512,512]{1,2,0:T(8,128)} %dynamic_update_slice.6, f32[5,256,256]{1,2,0:T(8,128)S(1)} %fusion, s32[]{:T(128)} %constant.40.clone.1, s32[]{:T(128)S(6)} %select_n.83, s32[]{:T(128)S(6)} %select_n.84) | dynamic-update-slice | bytes 2621444 | tf_op jit(solution)/shard_map/dynamic_update_slice | solution.py:112
  98.9 2.0 %fusion.31 = (f32[5,128,512]{1,2,0:T(8,128)S(1)}, f32[5,128,512]{1,2,0:T(8,128)S(1)}) fusion(f32[5,512,512]{1,2,0:T(8,128)} %dynamic_update_slice.7), kind=kLoop, calls=%fused_computation.81 | loop fusion | bytes 5242880 | tf_op jit(solution)/shard_map/slice | solution.py:115
  101.0 4.1 %collective-permute-start.4 = (f32[5,128,512]{1,2,0:T(8,128)S(1)}, f32[5,128,512]{1,2,0:T(8,128)S(1)}, u32[]{:S(2)}, u32[]{:S(2)}) collective-permute-start(f32[5,128,512]{1,2,0:T(8,128)S(1)} %get-tuple-element.5), channel_id=1, source_target_pairs={{0,1},{1,2},{2,3},{3,4},{4,5},{5,6},{6,7},{7,8},{8,9},{9,10},{10,1... | collective-permute-start | bytes 3932168 | tf_op jit(solution)/shard_map/ppermute | solution.py:28
  105.1 2.0 %collective-permute-start.5 = (f32[5,128,512]{1,2,0:T(8,128)S(1)}, f32[5,128,512]{1,2,0:T(8,128)S(1)}, u32[]{:S(2)}, u32[]{:S(2)}) collective-permute-start(f32[5,128,512]{1,2,0:T(8,128)S(1)} %get-tuple-element.6), channel_id=1, source_target_pairs={{1,0},{2,1},{3,2},{4,3},{5,4},{6,5},{7,6},{8,7},{9,8},{10,9},{11,1... | collective-permute-start | bytes 3932168 | tf_op jit(solution)/shard_map/ppermute | solution.py:28
  107.1 34.7 %collective-permute-done.4 = f32[5,128,512]{1,2,0:T(8,128)S(1)} collective-permute-done((f32[5,128,512]{1,2,0:T(8,128)S(1)}, f32[5,128,512]{1,2,0:T(8,128)S(1)}, u32[]{:S(2)}, u32[]{:S(2)}) %collective-permute-start.4) | collective-permute-done | bytes 1310752 | tf_op jit(solution)/shard_map/ppermute | solution.py:28
  141.8 0.0 collective-permute-done.5
  141.8 0.4 slice_add_fusion
  142.2 0.1 fusion.32
  142.3 14.0 %collective-permute-start.6 = (f32[5,256,128]{1,2,0:T(8,128)S(1)}, f32[5,256,128]{1,2,0:T(8,128)S(1)}, u32[]{:S(2)}, u32[]{:S(2)}) collective-permute-start(f32[5,256,128]{1,2,0:T(8,128)S(1)} %get-tuple-element.7), channel_id=1, source_target_pairs={{0,32},{32,64},{64,96},{96,128},{128,160},{160,192},{192,224},{224... | collective-permute-start | bytes 1966088 | tf_op jit(solution)/shard_map/ppermute | solution.py:28
  156.3 1.9 %collective-permute-start.7 = (f32[5,256,128]{1,2,0:T(8,128)S(1)}, f32[5,256,128]{1,2,0:T(8,128)S(1)}, u32[]{:S(2)}, u32[]{:S(2)}) collective-permute-start(f32[5,256,128]{1,2,0:T(8,128)S(1)} %get-tuple-element.8), channel_id=1, source_target_pairs={{32,0},{64,32},{96,64},{128,96},{160,128},{192,160},{224,192},{256... | collective-permute-start | bytes 1966088 | tf_op jit(solution)/shard_map/ppermute | solution.py:28
  158.3 13.0 %collective-permute-done.6 = f32[5,256,128]{1,2,0:T(8,128)S(1)} collective-permute-done((f32[5,256,128]{1,2,0:T(8,128)S(1)}, f32[5,256,128]{1,2,0:T(8,128)S(1)}, u32[]{:S(2)}, u32[]{:S(2)}) %collective-permute-start.6) | collective-permute-done | bytes 655392 | tf_op jit(solution)/shard_map/ppermute | solution.py:28
  171.2 4.3 %collective-permute-done.7 = f32[5,256,128]{1,2,0:T(8,128)S(1)} collective-permute-done((f32[5,256,128]{1,2,0:T(8,128)S(1)}, f32[5,256,128]{1,2,0:T(8,128)S(1)}, u32[]{:S(2)}, u32[]{:S(2)}) %collective-permute-start.7) | collective-permute-done | bytes 655392 | tf_op jit(solution)/shard_map/ppermute | solution.py:28
  175.6 0.2 slice_add_fusion.1
  175.9 0.1 slice.150
  175.9 0.3 copy.16
  176.3 0.1 copy.15
  176.4 2.4 %divide_subtract_fusion = f32[2,2,256,256]{3,2,1,0:T(8,128)} fusion(f32[2,2,256,256]{3,2,1,0:T(8,128)} %param.5, f32[2,2,256,256]{3,2,1,0:T(8,128)S(1)} %copy.16, f32[256,256]{1,0:T(8,128)S(1)} %copy.15), kind=kLoop, calls=%fused_computation.25 | loop fusion | flops 524288 | bytes 3407872 | tf_op jit(solution)/shard_map/sub | solution.py:125
  (38 shorter events, 0.2 us)
Async XLA Ops:
  0.0 16.1 %copy-start = (bf16[2,1,2,256,256]{4,3,2,1,0:T(8,128)(2,1)S(1)}, bf16[2,1,2,256,256]{4,3,2,1,0:T(8,128)(2,1)}, u32[]{:S(2)}) copy-start(bf16[2,1,2,256,256]{4,3,2,1,0:T(8,128)(2,1)} %param.8) | copy-start | bytes 1572868
  0.0 15.8 %copy-start.11 = (f32[2,256,256]{2,1,0:T(8,128)S(1)}, f32[2,256,256]{2,1,0:T(8,128)}, u32[]{:S(2)}) copy-start(f32[2,256,256]{2,1,0:T(8,128)} %param.6) | copy-start | bytes 1572868
  1.2 23.7 %copy-start.8 = (f32[2,256,256]{2,1,0:T(8,128)}, f32[2,256,256]{2,1,0:T(8,128)S(1)}, u32[]{:S(2)}) copy-start(f32[2,256,256]{2,1,0:T(8,128)S(1)} %slice_bitcast_fusion.2) | copy-start | bytes 1572868
  1.2 18.5 %collective-permute-start = (f32[2,256,128]{2,1,0:T(8,128)S(1)}, f32[2,256,128]{2,1,0:T(8,128)S(1)}, u32[]{:S(2)}, u32[]{:S(2)}) collective-permute-start(f32[2,256,128]{2,1,0:T(8,128)S(1)} %get-tuple-element.19), channel_id=1, source_target_pairs={{0,32},{32,64},{64,96},{96,128},{128,160},{160,192},{192,224},{224... | collective-permute-start | bytes 786440 | tf_op jit(solution)/shard_map/ppermute | solution.py:17
  7.0 17.8 %collective-permute-start.1 = (f32[2,256,128]{2,1,0:T(8,128)S(1)}, f32[2,256,128]{2,1,0:T(8,128)S(1)}, u32[]{:S(2)}, u32[]{:S(2)}) collective-permute-start(f32[2,256,128]{2,1,0:T(8,128)S(1)} %get-tuple-element.20), channel_id=1, source_target_pairs={{32,0},{64,32},{96,64},{128,96},{160,128},{192,160},{224,192},{256... | collective-permute-start | bytes 786440 | tf_op jit(solution)/shard_map/ppermute | solution.py:20
  16.0 3.0 %copy-start.2 = (f32[1,2,256,256]{2,3,1,0:T(8,128)}, f32[1,2,256,256]{2,3,1,0:T(8,128)S(1)}, u32[]{:S(2)}) copy-start(f32[1,2,256,256]{2,3,1,0:T(8,128)S(1)} %get-tuple-element.26) | copy-start | bytes 1572868
  16.1 3.0 %copy-start.4 = (f32[1,2,256,256]{2,3,0,1:T(8,128)}, f32[1,2,256,256]{2,3,0,1:T(8,128)S(1)}, u32[]{:S(2)}) copy-start(f32[1,2,256,256]{2,3,0,1:T(8,128)S(1)} %get-tuple-element.22) | copy-start | bytes 1572868
  16.1 3.0 %copy-start.6 = (f32[1,2,256,256]{2,3,0,1:T(8,128)}, f32[1,2,256,256]{2,3,0,1:T(8,128)S(1)}, u32[]{:S(2)}) copy-start(f32[1,2,256,256]{2,3,0,1:T(8,128)S(1)} %get-tuple-element.25) | copy-start | bytes 1572868
  17.1 1.9 %copy-start.18 = (s32[2,1,2]{2,1,0:T(1,128)S(1)}, s32[2,1,2]{2,1,0:T(1,128)}, u32[]{:S(2)}) copy-start(s32[2,1,2]{2,1,0:T(1,128)} %param.7) | copy-start | bytes 52
  19.8 18.9 %copy-start.17 = (bf16[2,1,2,256,256]{4,3,2,1,0:T(8,128)(2,1)S(1)}, bf16[2,1,2,256,256]{4,3,2,1,0:T(8,128)(2,1)}, u32[]{:S(2)}) copy-start(bf16[2,1,2,256,256]{4,3,2,1,0:T(8,128)(2,1)} %param.9) | copy-start | bytes 1572868
  19.8 6.3 %copy-start.15 = (f32[2,256,128]{2,1,0:T(8,128)}, f32[2,256,128]{2,1,0:T(8,128)S(1)}, u32[]{:S(2)}) copy-start(f32[2,256,128]{2,1,0:T(8,128)S(1)} %collective-permute-done) | copy-start | bytes 786436
  24.9 1.2 copy-start.16
  26.1 20.3 %collective-permute-start.2 = (f32[2,128,512]{2,1,0:T(8,128)}, f32[2,128,512]{2,1,0:T(8,128)}, u32[]{:S(2)}, u32[]{:S(2)}) collective-permute-start(f32[2,128,512]{2,1,0:T(8,128)} %get-tuple-element.15), channel_id=1, source_target_pairs={{0,1},{1,2},{2,3},{3,4},{4,5},{5,6},{6,7},{7,8},{8,9},{9,10},{10,1... | collective-permute-start | bytes 1572872 | tf_op jit(solution)/shard_map/ppermute | solution.py:17
  30.8 15.6 %collective-permute-start.3 = (f32[2,128,512]{2,1,0:T(8,128)}, f32[2,128,512]{2,1,0:T(8,128)}, u32[]{:S(2)}, u32[]{:S(2)}) collective-permute-start(f32[2,128,512]{2,1,0:T(8,128)} %get-tuple-element.16), channel_id=1, source_target_pairs={{1,0},{2,1},{3,2},{4,3},{5,4},{6,5},{7,6},{8,7},{9,8},{10,9},{11,1... | collective-permute-start | bytes 1572872 | tf_op jit(solution)/shard_map/ppermute | solution.py:20
  53.6 1.6 copy-start.5
  53.6 1.7 copy-start.7
  55.2 2.0 %copy-start.3 = (f32[1,2,256,256]{2,3,1,0:T(8,128)S(1)}, f32[1,2,256,256]{2,3,1,0:T(8,128)}, u32[]{:S(2)}) copy-start(f32[1,2,256,256]{2,3,1,0:T(8,128)} %copy-done.2) | copy-start | bytes 1572868
  57.2 1.9 %copy-start.13 = (f32[256,256]{0,1:T(8,128)S(1)}, f32[256,256]{0,1:T(8,128)}, u32[]{:S(2)}) copy-start(f32[256,256]{0,1:T(8,128)} %get-tuple-element.27) | copy-start | bytes 786436
  57.2 1.9 %copy-start.14 = (f32[256,256]{0,1:T(8,128)S(1)}, f32[256,256]{0,1:T(8,128)}, u32[]{:S(2)}) copy-start(f32[256,256]{0,1:T(8,128)} %get-tuple-element.28) | copy-start | bytes 786436
  61.1 1.9 %copy-start.10 = (f32[256,256]{0,1:T(8,128)S(1)}, f32[256,256]{0,1:T(8,128)}, u32[]{:S(2)}) copy-start(f32[256,256]{0,1:T(8,128)} %copy.11) | copy-start | bytes 786436
  63.2 1.0 copy-start.12
  64.2 1.5 copy-start.9
  98.9 42.9 %copy-start.1 = (f32[5,512,512]{1,2,0:T(8,128)S(1)}, f32[5,512,512]{1,2,0:T(8,128)}, u32[]{:S(2)}) copy-start(f32[5,512,512]{1,2,0:T(8,128)} %dynamic_update_slice.7) | copy-start | bytes 15728644
  101.0 40.8 %collective-permute-start.4 = (f32[5,128,512]{1,2,0:T(8,128)S(1)}, f32[5,128,512]{1,2,0:T(8,128)S(1)}, u32[]{:S(2)}, u32[]{:S(2)}) collective-permute-start(f32[5,128,512]{1,2,0:T(8,128)S(1)} %get-tuple-element.5), channel_id=1, source_target_pairs={{0,1},{1,2},{2,3},{3,4},{4,5},{5,6},{6,7},{7,8},{8,9},{9,10},{10,1... | collective-permute-start | bytes 3932168 | tf_op jit(solution)/shard_map/ppermute | solution.py:28
  105.1 36.7 %collective-permute-start.5 = (f32[5,128,512]{1,2,0:T(8,128)S(1)}, f32[5,128,512]{1,2,0:T(8,128)S(1)}, u32[]{:S(2)}, u32[]{:S(2)}) collective-permute-start(f32[5,128,512]{1,2,0:T(8,128)S(1)} %get-tuple-element.6), channel_id=1, source_target_pairs={{1,0},{2,1},{3,2},{4,3},{5,4},{6,5},{7,6},{8,7},{9,8},{10,9},{11,1... | collective-permute-start | bytes 3932168 | tf_op jit(solution)/shard_map/ppermute | solution.py:28
  142.3 28.9 %collective-permute-start.6 = (f32[5,256,128]{1,2,0:T(8,128)S(1)}, f32[5,256,128]{1,2,0:T(8,128)S(1)}, u32[]{:S(2)}, u32[]{:S(2)}) collective-permute-start(f32[5,256,128]{1,2,0:T(8,128)S(1)} %get-tuple-element.7), channel_id=1, source_target_pairs={{0,32},{32,64},{64,96},{96,128},{128,160},{160,192},{192,224},{224... | collective-permute-start | bytes 1966088 | tf_op jit(solution)/shard_map/ppermute | solution.py:28
  156.3 19.3 %collective-permute-start.7 = (f32[5,256,128]{1,2,0:T(8,128)S(1)}, f32[5,256,128]{1,2,0:T(8,128)S(1)}, u32[]{:S(2)}, u32[]{:S(2)}) collective-permute-start(f32[5,256,128]{1,2,0:T(8,128)S(1)} %get-tuple-element.8), channel_id=1, source_target_pairs={{32,0},{64,32},{96,64},{128,96},{160,128},{192,160},{224,192},{256... | collective-permute-start | bytes 1966088 | tf_op jit(solution)/shard_map/ppermute | solution.py:28
where the time goes:
time: 180 us; the launch traced here: 179 us
  waiting for transfers between devices  57.1 us (32%)
  local copies, waits for them, and re-layouts  47 us (26%)
  starting transfers between devices  41.2 us (23%)
  other arithmetic  14.9 us (8%)
  matrix products  10.4 us (6%)
  between operations  8.11 us (5%)
    ppermute x4, waiting for transfers between devices, from_behind(): lax.ppermute(value, axis, [(source, source + steps) for source in range(l...  52 us
    dynamic_update_slice x2, local copies, waits for them, and re-layouts, shards(): summed = lax.dynamic_update_slice(summed, current + planes[number], corner)  27.7 us
    ppermute x4, starting transfers between devices, from_behind(): lax.ppermute(value, axis, [(source, source + steps) for source in range(l...  22 us
    ppermute x2, starting transfers between devices, padded(): lax.ppermute(lax.slice_in_dim(block, block.shape[dim] - width, None, axis...  10.6 us
    ppermute x2, starting transfers between devices, padded(): lax.ppermute(lax.slice_in_dim(block, 0, width, axis=dim), axis, backward)  8.66 us
    dot_general x3, matrix products, transform(): jnp.einsum('pbjk,bakl->pajl', inner, right_table, precision=lax.Precision...  5.59 us
    dynamic_slice x3, local copies, waits for them, and re-layouts, shards(): lax.dynamic_slice(second_ext, (anchor, spots[number, 0], spots[number, 1]...  5.45 us
    ppermute x2, waiting for transfers between devices, padded(): lax.ppermute(lax.slice_in_dim(block, 0, width, axis=dim), axis, backward)  5.08 us
  transfers between devices with their start and end apart: 8, of which 4 were waited for; matrix products, arithmetic and copies ran while one was open for 7% of the time, Pallas kernels for 0%

commit v1 on v0

v1 whole, which is shorter than its diff:
```python
import functools
import math

import jax
import jax.numpy as jnp
import numpy as np
from jax import lax
from jax.experimental import pallas as pl
from jax.experimental.pallas import tpu as pltpu
from jax.sharding import PartitionSpec as P

fresnel_rate = 200.0
ridge = 0.5
WIN = 256
RIM = 128
MESH = pl.DeviceIdType.MESH
F32 = jnp.float32
BF16 = jnp.bfloat16

O_RIGHT, O_LEFT, O_DOWN, O_UP = 0, 1, 2, 3
OC_DOWN, OC_UP = 4, 6
POS_RIGHT, POS_LEFT, POS_DOWN, POS_UP = 8, 9, 10, 11
GRAD = 12
COPIES = GRAD + 16


def split(values):
    high = values.astype(BF16)
    return high, (values - high.astype(F32)).astype(BF16)


def constant_tables():
    index = np.arange(WIN)
    angle = (np.outer(index, index) % WIN) * (2.0 * math.pi / WIN)
    freq = ((index + WIN // 2) % WIN - WIN // 2) / WIN
    phase = fresnel_rate * freq**2
    inverse = np.exp(1j * angle) / math.sqrt(WIN)
    across = inverse @ np.diag(np.exp(1j * phase)) @ np.conj(inverse)

    def pieces(table):
        parts = [table.real, table.imag]
        high = [np.asarray(t, np.float32).astype(jnp.bfloat16) for t in parts]
        low = [(t - h.astype(np.float64)).astype(np.float32).astype(jnp.bfloat16) for t, h in zip(parts, high)]
        return np.stack(high + low)

    return pieces(inverse), pieces(across)


def dot(a, b):
    return jnp.dot(a, b, preferred_element_type=F32)


def kernel(
    rows,
    cols,
    pos_ref,
    obj_hbm,
    probe_hbm,
    res_hbm,
    sav_hbm,
    tab_hbm,
    atab_hbm,
    out_hbm,
    obj,
    probe,
    res,
    sav,
    tab,
    atab,
    ext,
    posx,
    posall,
    frame,
    from_up,
    from_down,
    from_left,
    from_right,
    side,
    left_tab,
    right_tab,
    left_a,
    right_a,
    fields,
    pair,
    big,
    gbuf,
    pbuf,
    lsq,
    light,
    obuf,
    send_sem,
    recv_sem,
    load_sem,
):
    gx = lax.axis_index("gx")
    gy = lax.axis_index("gy")
    right = {"gx": lax.rem(gx + 1, cols)}
    left = {"gx": lax.rem(gx + cols - 1, cols)}
    down = {"gy": lax.rem(gy + 1, rows)}
    up = {"gy": lax.rem(gy + rows - 1, rows)}

    loads = []

    def load(source, target):
        copy = pltpu.make_async_copy(source, target, load_sem.at[len(loads)])
        copy.start()
        loads.append(copy)

    load(res_hbm, res.at[:, 0:512])
    load(res_hbm, res.at[:, 512:1024])
    load(tab_hbm, tab)
    load(sav_hbm, sav)
    load(probe_hbm, probe)
    load(atab_hbm, atab)
    load(obj_hbm.at[1], ext.at[:, RIM : 3 * RIM, RIM : 3 * RIM])
    load(obj_hbm, obj)

    barrier = pltpu.get_barrier_semaphore()
    for neighbour in (left, right, up, down):
        pl.semaphore_signal(barrier, inc=1, device_id=neighbour, device_id_type=MESH)
    pl.semaphore_wait(barrier, 4)

    copies = {}

    def send(source, target, number, to):
        copy = pltpu.make_async_remote_copy(
            src_ref=source,
            dst_ref=target,
            send_sem=send_sem.at[number],
            recv_sem=recv_sem.at[number],
            device_id=to,
            device_id_type=MESH,
        )
        copy.start()
        copies[number] = copy

    def arrived(*numbers):
        for number in numbers:
            copies[number].wait_recv()

    send(obj_hbm.at[1, :, :, RIM:], ext.at[:, RIM : 3 * RIM, 0:RIM], O_RIGHT, right)
    send(obj_hbm.at[1, :, :, 0:RIM], ext.at[:, RIM : 3 * RIM, 3 * RIM :], O_LEFT, left)
    for number in range(2):
        for axis in range(2):
            value = pos_ref[number, axis].astype(F32)
            posx[1, 2 * number + axis : 2 * number + axis + 1, :] = jnp.full((1, 128), value, F32)
    posx[1, 4:8, :] = jnp.zeros((4, 128), F32)
    send(obj_hbm.at[1, :, RIM:, :], ext.at[:, 0:RIM, RIM : 3 * RIM], O_DOWN, down)
    send(obj_hbm.at[1, :, 0:RIM, :], ext.at[:, 3 * RIM :, RIM : 3 * RIM], O_UP, up)
    send(posx.at[1], posx.at[0], POS_RIGHT, right)
    send(posx.at[1], posx.at[2], POS_LEFT, left)

    row_index = lax.broadcasted_iota(jnp.int32, (WIN, WIN), 0)
    col_index = lax.broadcasted_iota(jnp.int32, (WIN, WIN), 1)

    def turn(shift):
        offset = row_index - col_index
        hit = (offset == shift) | (offset == shift - WIN)
        return jnp.where(hit, 1.0, 0.0).astype(BF16)

    def turn_columns(shift):
        offset = col_index - row_index
        hit = (offset == shift) | (offset == shift - WIN)
        return jnp.where(hit, 1.0, 0.0).astype(BF16)

    def place(target, field, row, col):
        for a in range(2):
            low = row_index >= row if a == 0 else row_index < row
            for b in range(2):
                hit = low & (col_index >= col if b == 0 else col_index < col)
                spot = (slice(a * WIN, (a + 1) * WIN), slice(b * WIN, (b + 1) * WIN))
                target[spot] = target[spot] + jnp.where(hit, field, 0.0)

    frame[...] = jnp.zeros_like(frame)
    for copy in loads:
        copy.wait()

    def first(number, carry):
        row = pos_ref[number, 0]
        col = pos_ref[number, 1]
        rows_turned = turn(row)
        cols_turned = turn_columns(col)
        for half in range(2):
            cos = dot(rows_turned, tab[2 * half])
            sin = dot(rows_turned, tab[2 * half + 1])
            at = 512 * half
            left_tab[0:256, at : at + 256] = cos.astype(BF16)
            left_tab[0:256, at + 256 : at + 512] = (-sin).astype(BF16)
            left_tab[256:512, at : at + 256] = sin.astype(BF16)
            left_tab[256:512, at + 256 : at + 512] = cos.astype(BF16)
            cos = dot(tab[2 * half], cols_turned)
            sin = dot(tab[2 * half + 1], cols_turned)
            for at in (0, 512) if half == 0 else (1024,):
                right_tab[at : at + 256, 0:256] = cos.astype(BF16)
                right_tab[at : at + 256, 256:512] = sin.astype(BF16)
                right_tab[at + 256 : at + 512, 0:256] = (-sin).astype(BF16)
                right_tab[at + 256 : at + 512, 256:512] = cos.astype(BF16)
        half_way = dot(left_tab[...], res[number])
        high, low = split(half_way)
        for part in range(2):
            span = slice(256 * part, 256 * part + 256)
            for at, piece in ((0, high), (512, low), (1024, high)):
                pair[0:256, at + 256 * part : at + 256 * part + 256] = piece[span]
        field = dot(pair[0:256, :], right_tab[...])
        gbuf[number] = field
        field_re = field[:, 0:256]
        field_im = field[:, 256:512]
        wave_re = dot(dot(rows_turned, sav[number, 0]).astype(BF16), cols_turned)
        wave_im = dot(dot(rows_turned, sav[number, 1]).astype(BF16), cols_turned)
        place(frame.at[0, 0], wave_re * field_re + wave_im * field_im, row, col)
        place(frame.at[0, 1], wave_re * field_im - wave_im * field_re, row, col)
        for part in range(2):
            high, low = split(probe[part])
            high = dot(dot(rows_turned, high).astype(BF16), cols_turned)
            low = dot(dot(rows_turned, low).astype(BF16), cols_turned)
            pbuf[number, part] = high + low
        return carry

    lax.fori_loop(0, 2, first, 0)

    for half in range(2):
        real = atab[2 * half]
        imag = atab[2 * half + 1]
        for at in (0, 512) if half == 0 else (1024,):
            left_a[0:256, at : at + 256] = real
            left_a[0:256, at + 256 : at + 512] = -imag
            left_a[256:512, at : at + 256] = imag
            left_a[256:512, at + 256 : at + 512] = real
            right_a[at : at + 256, 0:256] = real
            right_a[at : at + 256, 256:512] = imag
            right_a[at + 256 : at + 512, 0:256] = -imag
            right_a[at + 256 : at + 512, 256:512] = real
    high, low = split(probe[0] * probe[0] + probe[1] * probe[1])
    lsq[0] = high
    lsq[1] = low

    def send_rows(group):
        base = GRAD + 8 * group
        for v, at in ((0, 0), (1, 3 * RIM)):
            send(
                frame.at[group, :, 3 * RIM :, at : at + RIM],
                from_up.at[group, :, :, at : at + RIM],
                base + v,
                down,
            )
            send(
                frame.at[group, :, 0:RIM, at : at + RIM],
                from_down.at[group, :, :, at : at + RIM],
                base + 2 + v,
                up,
            )
        centre = slice(RIM, 3 * RIM)
        send(frame.at[group, :, 3 * RIM :, centre], from_up.at[group, :, :, centre], base + 4, down)
        send(frame.at[group, :, 0:RIM, centre], from_down.at[group, :, :, centre], base + 5, up)

    def drop_rows(group, spans):
        @pl.when(gy == 0)
        def _():
            for span in spans:
                from_up[group, :, :, span] = jnp.zeros((2, RIM, span.stop - span.start), F32)

        @pl.when(gy == rows - 1)
        def _():
            for span in spans:
                from_down[group, :, :, span] = jnp.zeros((2, RIM, span.stop - span.start), F32)

    def send_sides(group):
        base = GRAD + 8 * group
        arrived(base, base + 1, base + 2, base + 3)
        drop_rows(group, (slice(0, RIM), slice(3 * RIM, 4 * RIM)))
        for which, at in ((0, 3 * RIM), (1, 0)):
            span = slice(at, at + RIM)
            side[group, which, :, 0:RIM] = frame[group, :, RIM : 2 * RIM, span] + from_up[group, :, :, span]
            side[group, which, :, RIM:] = frame[group, :, 2 * RIM : 3 * RIM, span] + from_down[group, :, :, span]
        send(side.at[group, 0], from_left.at[group], base + 6, right)
        send(side.at[group, 1], from_right.at[group], base + 7, left)

    def finish(group):
        base = GRAD + 8 * group
        arrived(base + 4, base + 5)
        drop_rows(group, (slice(RIM, 3 * RIM),))
        arrived(base + 6, base + 7)

        @pl.when(gx == 0)
        def _():
            from_left[group] = jnp.zeros((2, WIN, RIM), F32)

        @pl.when(gx == cols - 1)
        def _():
            from_right[group] = jnp.zeros((2, WIN, RIM), F32)

        for part in range(2):
            for h, vertical in ((0, from_up), (1, from_down)):
                for v, horizontal in ((0, from_left), (1, from_right)):
                    tall = slice(h * RIM, h * RIM + RIM)
                    wide = slice(v * RIM, v * RIM + RIM)
                    total = (
                        frame[group, part, RIM + h * RIM : 2 * RIM + h * RIM, RIM + v * RIM : 2 * RIM + v * RIM]
                        + vertical[group, part, :, RIM + v * RIM : 2 * RIM + v * RIM]
                        + horizontal[group, part, tall, :]
                    )
                    obuf[1 - group, part, tall, wide] = obj[1 - group, part, tall, wide] - total / light[tall, wide]
        copy = pltpu.make_async_copy(obuf.at[1 - group], out_hbm.at[1 - group], load_sem.at[8 + group])
        copy.start()
        return copy

    arrived(O_RIGHT, O_LEFT)
    for v, at in ((0, 0), (1, 3 * RIM)):
        span = slice(at, at + RIM)
        send(ext.at[:, 2 * RIM : 3 * RIM, span], ext.at[:, 0:RIM, span], OC_DOWN + v, down)
        send(ext.at[:, RIM : 2 * RIM, span], ext.at[:, 3 * RIM :, span], OC_UP + v, up)
    arrived(POS_RIGHT, POS_LEFT)
    posall[1] = posx[...]
    send(posx, posall.at[0], POS_DOWN, down)
    send(posx, posall.at[2], POS_UP, up)
    send_rows(0)

    light[...] = jnp.full((WIN, WIN), ridge, F32)
    arrived(POS_DOWN, POS_UP)
    offset = (row_index - col_index).astype(F32)

    def lit(number, carry):
        dy = number // 3 - 1
        dx = number % 3 - 1
        inside = (gy + dy >= 0) & (gy + dy < rows) & (gx + dx >= 0) & (gx + dx < cols)
        weight = jnp.where(inside, 1.0, 0.0)
        spots = posall[number // 3, number % 3]
        total = light[...]
        for spot in range(2):
            row = spots[2 * spot : 2 * spot + 1, :] + (dy * WIN - RIM).astype(F32)
            col = spots[2 * spot + 1 : 2 * spot + 2, :] + (dx * WIN - RIM).astype(F32)
            row = jnp.concatenate([row, row], axis=1)
            col = jnp.concatenate([col, col], axis=1)
            by_rows = jnp.where(offset == row, weight, 0.0).astype(BF16)
            by_cols = jnp.where(-offset == col, 1.0, 0.0).astype(BF16)
            for part in range(2):
                total = total + dot(by_rows, dot(lsq[part], by_cols).astype(BF16))
        light[...] = total
        return carry

    lax.fori_loop(0, 9, lit, 0)

    arrived(O_DOWN, O_UP, OC_DOWN, OC_DOWN + 1, OC_UP, OC_UP + 1)

    first_row = jnp.where(gy == 0, RIM, 0)
    last_row = jnp.where(gy == rows - 1, 3 * RIM, 4 * RIM)
    first_col = jnp.where(gx == 0, RIM, 0)
    last_col = jnp.where(gx == cols - 1, 3 * RIM, 4 * RIM)

    for number in range(2):
        row = pos_ref[number, 0]
        col = pos_ref[number, 1]
        upper = row_index >= row
        leftmost = col_index >= col
        at_row = jnp.where(upper, row_index, row_index + WIN)
        at_col = jnp.where(leftmost, col_index, col_index + WIN)
        inside = (at_row >= first_row) & (at_row < last_row) & (at_col >= first_col) & (at_col < last_col)
        patch = []
        for part in range(2):
            top = jnp.where(leftmost, ext[part, 0:256, 0:256], ext[part, 0:256, 256:512])
            bottom = jnp.where(leftmost, ext[part, 256:512, 0:256], ext[part, 256:512, 256:512])
            patch.append(jnp.where(inside, jnp.where(upper, top, bottom), 0.0))
        field_re = gbuf[number, :, 0:256]
        field_im = gbuf[number, :, 256:512]
        chi = (
            patch[0] * field_re + patch[1] * field_im,
            patch[0] * field_im - patch[1] * field_re,
        )
        for part in range(2):
            high, low = split(chi[part])
            for at, piece in ((0, high), (512, low), (1024, high)):
                fields[at + 256 * part : at + 256 * part + 256, 256 * number : 256 * number + 256] = piece
    big[...] = dot(left_a[...], fields[...])
    for number in range(2):
        for part in range(2):
            high, low = split(big[256 * part : 256 * part + 256, 256 * number : 256 * number + 256])
            for at, piece in ((0, high), (512, low), (1024, high)):
                pair[256 * number : 256 * number + 256, at + 256 * part : at + 256 * part + 256] = piece
    big[...] = dot(pair[...], right_a[...])

    def second(number, carry):
        row = pos_ref[number, 0]
        col = pos_ref[number, 1]
        span = pl.ds(pl.multiple_of(number * 256, 256), 256)
        back_re = big[span, 0:256]
        back_im = big[span, 256:512]
        probe_re = pbuf[number, 0]
        probe_im = pbuf[number, 1]
        place(frame.at[1, 0], probe_re * back_re + probe_im * back_im, row, col)
        place(frame.at[1, 1], probe_re * back_im - probe_im * back_re, row, col)
        return carry

    lax.fori_loop(0, 2, second, 0)
    send_sides(0)
    send_rows(1)
    send_sides(1)
    stores = [finish(0), finish(1)]
    for copy in stores:
        copy.wait()
    for number in range(COPIES):
        copies[number].wait_send()


def solution(mesh):
    rows, cols = mesh.shape["gy"], mesh.shape["gx"]
    tab, atab = constant_tables()

    def step(object_field, probe, positions, residual, saved_wave):
        anywhere = pl.BlockSpec(memory_space=pl.ANY)
        vmem = pltpu.VMEM
        return pl.pallas_call(
            functools.partial(kernel, rows, cols),
            name="adjoint",
            out_shape=jax.ShapeDtypeStruct((2, 2, WIN, WIN), F32),
            in_specs=[pl.BlockSpec(memory_space=pltpu.SMEM)] + [anywhere] * 6,
            out_specs=anywhere,
            scratch_shapes=[
                vmem((2, 2, WIN, WIN), F32),
                vmem((2, WIN, WIN), F32),
                vmem((2, 1024, WIN), BF16),
                vmem((2, 2, WIN, WIN), BF16),
                vmem((4, WIN, WIN), BF16),
                vmem((4, WIN, WIN), BF16),
                vmem((2, 512, 512), F32),
                vmem((3, 8, 128), F32),
                vmem((3, 3, 8, 128), F32),
                vmem((2, 2, 512, 512), F32),
                vmem((2, 2, RIM, 512), F32),
                vmem((2, 2, RIM, 512), F32),
                vmem((2, 2, WIN, RIM), F32),
                vmem((2, 2, WIN, RIM), F32),
                vmem((2, 2, 2, WIN, RIM), F32),
                vmem((512, 1024), BF16),
                vmem((1536, 512), BF16),
                vmem((512, 1536), BF16),
                vmem((1536, 512), BF16),
                vmem((1536, 512), BF16),
                vmem((512, 1536), BF16),
                vmem((512, 512), F32),
                vmem((2, WIN, 512), F32),
                vmem((2, 2, WIN, WIN), F32),
                vmem((2, WIN, WIN), BF16),
                vmem((WIN, WIN), F32),
                vmem((2, 2, WIN, WIN), F32),
                pltpu.SemaphoreType.DMA((COPIES,)),
                pltpu.SemaphoreType.DMA((COPIES,)),
                pltpu.SemaphoreType.DMA((10,)),
            ],
            compiler_params=pltpu.CompilerParams(
                collective_id=0, has_side_effects=True, vmem_limit_bytes=56 * 1024 * 1024
            ),
        )(
            positions.reshape(2, 2),
            object_field,
            probe,
            residual.reshape(2, 512, WIN),
            saved_wave.reshape(2, 2, WIN, WIN),
            jnp.asarray(tab),
            jnp.asarray(atab),
        )

    placed = (
        P(None, None, "gy", "gx"),
        P(),
        P("gy", "gx", None),
        P("gy", "gx", None, None, None),
        P("gy", "gx", None, None, None),
    )
    return jax.shard_map(
        step, mesh=mesh, in_specs=placed, out_specs=P(None, None, "gy", "gx"), check_vma=False
    )
```

time: 180 us -> 88 us (0.49)
  the two profiles are of different devices: /device:TPU:37 before, /device:TPU:1 now
where the time goes in v1:
time: 88 us; the launch traced here: 87.8 us
  Pallas kernels  85.5 us (97%)
  local copies, waits for them, and re-layouts  2.29 us (3%)
    pallas_call x1, Pallas kernels, step(): pl.pallas_call(functools.partial(kernel, rows, cols), name='adjoint', out...  85.5 us
    unnamed x1, local copies, waits for them, and re-layouts  2.29 us

profile of v1, /device:TPU:1, one launch (start us, length us, event | category | flops | bytes accessed | tf_op | source)
XLA Modules:
  0.0 87.8 jit_solution(3620487729601622254)
XLA Ops:
  0.0 85.5 %adjoint.1 = f32[2,2,256,256]{3,2,1,0:T(8,128)} custom-call(s32[2,2]{1,0:T(2,128)} %bitcast.5, f32[2,2,256,256]{3,2,1,0:T(8,128)} %obj_hbm.1, f32[2,256,256]{2,1,0:T(8,128)} %probe_hbm.1, bf16[2,512,256]{2,1,0:T(8,128)(2,1)} %bitcast.3, bf16[2,2,256,256]{3,2,1,0:T(8,128)(2,1)} %bitcast.4, bf16[4,256,256]{2,1,0:T(8,128)(2,1)} %constant.4.clone.tab_hbm, ...), custom_call_target="tpu_custom_call" | custom-call | tf_op jit(solution)/shard_map/adjoint/pallas_call | solution.py:411
  85.5 2.3 %copy.9 = f32[2,2,256,256]{3,2,1,0:T(8,128)} copy(f32[2,2,256,256]{3,2,1,0:T(8,128)} %adjoint.1) | data formatting | bytes 2097152

commit v2 on v1

--- a/solution.py
+++ b/solution.py
@@ -17,11 +17,12 @@
 F32 = jnp.float32
 BF16 = jnp.bfloat16
 
-O_RIGHT, O_LEFT, O_DOWN, O_UP = 0, 1, 2, 3
-OC_DOWN, OC_UP = 4, 6
-POS_RIGHT, POS_LEFT, POS_DOWN, POS_UP = 8, 9, 10, 11
-GRAD = 12
-COPIES = GRAD + 16
+O_RIGHT, O_LEFT = 0, 1
+C_INNER, C_STRAIGHT, C_DIAGONAL, C_EDGE = 2, 3, 4, 5
+H_INNER, H_STRAIGHT, H_DIAGONAL = 6, 8, 9
+POS_RIGHT, POS_LEFT, POS_INNER, POS_OUTER = 10, 11, 12, 13
+GRAD = 14
+COPIES = GRAD + 12
 
 
 def split(values):
@@ -71,8 +72,10 @@
     posx,
     posall,
     frame,
-    from_up,
-    from_down,
+    within,
+    straight,
+    slanted,
+    edge,
     from_left,
     from_right,
     side,
@@ -94,10 +97,24 @@
 ):
     gx = lax.axis_index("gx")
     gy = lax.axis_index("gy")
+    core = gy % 2
+    parity = (gy // 2) % 2
+    out_row = gy - 1 + 2 * core
+    side_col = gx - 1 + 2 * parity
+    has_left, has_right = gx > 0, gx < cols - 1
+    has_outer = (out_row >= 0) & (out_row < rows)
+    has_side = (side_col >= 0) & (side_col < cols)
+    has_diagonal = has_outer & has_side
+    lone = has_outer & jnp.logical_not(has_side)
+    facing = has_outer & (((gx == 0) & (parity == 1)) | ((gx == cols - 1) & (parity == 0)))
     right = {"gx": lax.rem(gx + 1, cols)}
     left = {"gx": lax.rem(gx + cols - 1, cols)}
-    down = {"gy": lax.rem(gy + 1, rows)}
-    up = {"gy": lax.rem(gy + rows - 1, rows)}
+    inner = {"gy": gy + 1 - 2 * core}
+    outer = {"gy": lax.rem(out_row + rows, rows)}
+    diagonal = {"gx": lax.rem(side_col + cols, cols), "gy": lax.rem(out_row + rows, rows)}
+
+    def cut(start, size=RIM):
+        return pl.ds(pl.multiple_of(start, RIM), size)
 
     loads = []
 
@@ -115,14 +132,30 @@
     load(obj_hbm.at[1], ext.at[:, RIM : 3 * RIM, RIM : 3 * RIM])
     load(obj_hbm, obj)
 
+    frame[...] = jnp.zeros_like(frame)
+
+    @pl.when(gx == 0)
+    def _():
+        ext[:, RIM : 3 * RIM, 0:RIM] = jnp.zeros((2, WIN, RIM), F32)
+
+    @pl.when(gx == cols - 1)
+    def _():
+        ext[:, RIM : 3 * RIM, 3 * RIM :] = jnp.zeros((2, WIN, RIM), F32)
+
     barrier = pltpu.get_barrier_semaphore()
-    for neighbour in (left, right, up, down):
-        pl.semaphore_signal(barrier, inc=1, device_id=neighbour, device_id_type=MESH)
-    pl.semaphore_wait(barrier, 4)
+    greeted = 1
+    pl.semaphore_signal(barrier, inc=1, device_id=inner, device_id_type=MESH)
+    for there, who in ((has_left, left), (has_right, right), (has_outer, outer), (has_diagonal, diagonal)):
+        @pl.when(there)
+        def _():
+            pl.semaphore_signal(barrier, inc=1, device_id=who, device_id_type=MESH)
+
+        greeted = greeted + there.astype(jnp.int32)
+    pl.semaphore_wait(barrier, greeted)
 
     copies = {}
 
-    def send(source, target, number, to):
+    def send(source, target, number, to, there=None, comes=None):
         copy = pltpu.make_async_remote_copy(
             src_ref=source,
             dst_ref=target,
@@ -131,24 +164,54 @@
             device_id=to,
             device_id_type=MESH,
         )
-        copy.start()
-        copies[number] = copy
+        comes = there if comes is None else comes
+        copies[number] = (copy, there, comes)
+        if there is None:
+            copy.start()
+        else:
+            pl.when(there)(copy.start)
 
     def arrived(*numbers):
         for number in numbers:
-            copies[number].wait_recv()
-
-    send(obj_hbm.at[1, :, :, RIM:], ext.at[:, RIM : 3 * RIM, 0:RIM], O_RIGHT, right)
-    send(obj_hbm.at[1, :, :, 0:RIM], ext.at[:, RIM : 3 * RIM, 3 * RIM :], O_LEFT, left)
+            copy, _, comes = copies[number]
+            if comes is None:
+                copy.wait_recv()
+            else:
+                pl.when(comes)(copy.wait_recv)
+
+    send(obj_hbm.at[1, :, :, RIM:], ext.at[:, RIM : 3 * RIM, 0:RIM], O_RIGHT, right, has_right, has_left)
+    send(obj_hbm.at[1, :, :, 0:RIM], ext.at[:, RIM : 3 * RIM, 3 * RIM :], O_LEFT, left, has_left, has_right)
+    near = 128 * parity
+    halo = 384 * parity
+    over = WIN * (1 - 2 * parity)
+    below = RIM * core
+    above = RIM - RIM * core
+    outside = 3 * RIM * (1 - core)
+    inside_row = 3 * RIM * core
+    send(obj_hbm.at[1, :, cut(below), cut(near)], ext.at[:, cut(outside), cut(RIM + near)], C_STRAIGHT, outer, has_outer)
+    send(
+        obj_hbm.at[1, :, cut(below), cut(near)],
+        ext.at[:, cut(outside), cut(RIM + near + over)],
+        C_DIAGONAL,
+        diagonal,
+        has_diagonal,
+    )
+    send(
+        obj_hbm.at[1, :, cut(below), cut(RIM - near)],
+        ext.at[:, cut(outside), cut(WIN - near)],
+        C_EDGE,
+        outer,
+        facing,
+        lone,
+    )
+    send(obj_hbm.at[1, :, cut(above), :], ext.at[:, cut(inside_row), RIM : 3 * RIM], C_INNER, inner)
     for number in range(2):
         for axis in range(2):
             value = pos_ref[number, axis].astype(F32)
             posx[1, 2 * number + axis : 2 * number + axis + 1, :] = jnp.full((1, 128), value, F32)
     posx[1, 4:8, :] = jnp.zeros((4, 128), F32)
-    send(obj_hbm.at[1, :, RIM:, :], ext.at[:, 0:RIM, RIM : 3 * RIM], O_DOWN, down)
-    send(obj_hbm.at[1, :, 0:RIM, :], ext.at[:, 3 * RIM :, RIM : 3 * RIM], O_UP, up)
-    send(posx.at[1], posx.at[0], POS_RIGHT, right)
-    send(posx.at[1], posx.at[2], POS_LEFT, left)
+    send(posx.at[1], posx.at[0], POS_RIGHT, right, has_right, has_left)
+    send(posx.at[1], posx.at[2], POS_LEFT, left, has_left, has_right)
 
     row_index = lax.broadcasted_iota(jnp.int32, (WIN, WIN), 0)
     col_index = lax.broadcasted_iota(jnp.int32, (WIN, WIN), 1)
@@ -171,7 +234,6 @@
                 spot = (slice(a * WIN, (a + 1) * WIN), slice(b * WIN, (b + 1) * WIN))
                 target[spot] = target[spot] + jnp.where(hit, field, 0.0)
 
-    frame[...] = jnp.zeros_like(frame)
     for copy in loads:
         copy.wait()
 
@@ -235,51 +297,37 @@
     lsq[1] = low
 
     def send_rows(group):
-        base = GRAD + 8 * group
-        for v, at in ((0, 0), (1, 3 * RIM)):
-            send(
-                frame.at[group, :, 3 * RIM :, at : at + RIM],
-                from_up.at[group, :, :, at : at + RIM],
-                base + v,
-                down,
-            )
-            send(
-                frame.at[group, :, 0:RIM, at : at + RIM],
-                from_down.at[group, :, :, at : at + RIM],
-                base + 2 + v,
-                up,
-            )
-        centre = slice(RIM, 3 * RIM)
-        send(frame.at[group, :, 3 * RIM :, centre], from_up.at[group, :, :, centre], base + 4, down)
-        send(frame.at[group, :, 0:RIM, centre], from_down.at[group, :, :, centre], base + 5, up)
-
-    def drop_rows(group, spans):
-        @pl.when(gy == 0)
-        def _():
-            for span in spans:
-                from_up[group, :, :, span] = jnp.zeros((2, RIM, span.stop - span.start), F32)
-
-        @pl.when(gy == rows - 1)
-        def _():
-            for span in spans:
-                from_down[group, :, :, span] = jnp.zeros((2, RIM, span.stop - span.start), F32)
+        base = GRAD + 6 * group
+        send(frame.at[group, :, cut(3 * RIM * core), cut(WIN - WIN * parity, WIN)], straight.at[group], base + 1, outer, has_outer)
+        send(frame.at[group, :, cut(3 * RIM * core), cut(WIN * parity, WIN)], slanted.at[group], base + 2, diagonal, has_diagonal)
+        send(frame.at[group, :, cut(3 * RIM * core), cut(RIM + near)], edge.at[group], base + 3, outer, lone, facing)
+        send(frame.at[group, :, cut(3 * RIM - 3 * RIM * core), :], within.at[group], base, inner)
 
     def send_sides(group):
-        base = GRAD + 8 * group
+        base = GRAD + 6 * group
         arrived(base, base + 1, base + 2, base + 3)
-        drop_rows(group, (slice(0, RIM), slice(3 * RIM, 4 * RIM)))
-        for which, at in ((0, 3 * RIM), (1, 0)):
-            span = slice(at, at + RIM)
-            side[group, which, :, 0:RIM] = frame[group, :, RIM : 2 * RIM, span] + from_up[group, :, :, span]
-            side[group, which, :, RIM:] = frame[group, :, 2 * RIM : 3 * RIM, span] + from_down[group, :, :, span]
-        send(side.at[group, 0], from_left.at[group], base + 6, right)
-        send(side.at[group, 1], from_right.at[group], base + 7, left)
+        for part in range(2):
+            spot = (group, part, cut(WIN - RIM * core), slice(None))
+            frame[spot] = frame[spot] + within[group, part]
+            spot = (group, part, cut(RIM + RIM * core), cut(WIN * parity, WIN))
+            for there, piece in ((has_outer, straight), (has_diagonal, slanted)):
+                @pl.when(there)
+                def _():
+                    frame[spot] = frame[spot] + piece[group, part]
+
+            @pl.when(facing)
+            def _():
+                spot = (group, part, cut(RIM + RIM * core), cut(WIN - near))
+                frame[spot] = frame[spot] + edge[group, part]
+
+        middle = slice(RIM, 3 * RIM)
+        side[group, 0] = frame[group, :, middle, 3 * RIM :]
+        side[group, 1] = frame[group, :, middle, 0:RIM]
+        send(side.at[group, 0], from_left.at[group], base + 4, right, has_right, has_left)
+        send(side.at[group, 1], from_right.at[group], base + 5, left, has_left, has_right)
 
     def finish(group):
-        base = GRAD + 8 * group
-        arrived(base + 4, base + 5)
-        drop_rows(group, (slice(RIM, 3 * RIM),))
-        arrived(base + 6, base + 7)
+        base = GRAD + 6 * group
 
         @pl.when(gx == 0)
         def _():
@@ -289,34 +337,33 @@
         def _():
             from_right[group] = jnp.zeros((2, WIN, RIM), F32)
 
-        for part in range(2):
-            for h, vertical in ((0, from_up), (1, from_down)):
-                for v, horizontal in ((0, from_left), (1, from_right)):
-                    tall = slice(h * RIM, h * RIM + RIM)
-                    wide = slice(v * RIM, v * RIM + RIM)
-                    total = (
-                        frame[group, part, RIM + h * RIM : 2 * RIM + h * RIM, RIM + v * RIM : 2 * RIM + v * RIM]
-                        + vertical[group, part, :, RIM + v * RIM : 2 * RIM + v * RIM]
-                        + horizontal[group, part, tall, :]
-                    )
-                    obuf[1 - group, part, tall, wide] = obj[1 - group, part, tall, wide] - total / light[tall, wide]
+        arrived(base + 4, base + 5)
+        for part in range(2):
+            for v, horizontal in ((0, from_left), (1, from_right)):
+                wide = slice(v * RIM, v * RIM + RIM)
+                total = (
+                    frame[group, part, RIM : 3 * RIM, RIM + v * RIM : 2 * RIM + v * RIM]
+                    + horizontal[group, part]
+                )
+                obuf[1 - group, part, :, wide] = obj[1 - group, part, :, wide] - total / light[:, wide]
         copy = pltpu.make_async_copy(obuf.at[1 - group], out_hbm.at[1 - group], load_sem.at[8 + group])
         copy.start()
         return copy
 
     arrived(O_RIGHT, O_LEFT)
-    for v, at in ((0, 0), (1, 3 * RIM)):
-        span = slice(at, at + RIM)
-        send(ext.at[:, 2 * RIM : 3 * RIM, span], ext.at[:, 0:RIM, span], OC_DOWN + v, down)
-        send(ext.at[:, RIM : 2 * RIM, span], ext.at[:, 3 * RIM :, span], OC_UP + v, up)
+    rows_out, rows_in = cut(RIM + below), cut(RIM + above)
+    send(ext.at[:, rows_out, cut(halo)], ext.at[:, cut(outside), cut(halo)], H_STRAIGHT, outer, has_outer)
+    send(ext.at[:, rows_out, cut(halo)], ext.at[:, cut(outside), cut(halo + over)], H_DIAGONAL, diagonal, has_diagonal)
+    for v, span in ((0, slice(0, RIM)), (1, slice(3 * RIM, 4 * RIM))):
+        send(ext.at[:, rows_in, span], ext.at[:, cut(inside_row), span], H_INNER + v, inner)
     arrived(POS_RIGHT, POS_LEFT)
     posall[1] = posx[...]
-    send(posx, posall.at[0], POS_DOWN, down)
-    send(posx, posall.at[2], POS_UP, up)
+    send(posx, posall.at[2 - 2 * (1 - core)], POS_INNER, inner)
+    send(posx, posall.at[2 - 2 * core], POS_OUTER, outer, has_outer)
     send_rows(0)
 
     light[...] = jnp.full((WIN, WIN), ridge, F32)
-    arrived(POS_DOWN, POS_UP)
+    arrived(POS_INNER, POS_OUTER)
     offset = (row_index - col_index).astype(F32)
 
     def lit(number, carry):
@@ -340,7 +387,7 @@
 
     lax.fori_loop(0, 9, lit, 0)
 
-    arrived(O_DOWN, O_UP, OC_DOWN, OC_DOWN + 1, OC_UP, OC_UP + 1)
+    arrived(C_INNER, C_STRAIGHT, C_DIAGONAL, C_EDGE, H_INNER, H_INNER + 1, H_STRAIGHT, H_DIAGONAL)
 
     first_row = jnp.where(gy == 0, RIM, 0)
     last_row = jnp.where(gy == rows - 1, 3 * RIM, 4 * RIM)
@@ -391,14 +438,18 @@
         return carry
 
     lax.fori_loop(0, 2, second, 0)
+    send_rows(1)
     send_sides(0)
-    send_rows(1)
     send_sides(1)
     stores = [finish(0), finish(1)]
     for copy in stores:
         copy.wait()
     for number in range(COPIES):
-        copies[number].wait_send()
+        copy, there, _ = copies[number]
+        if there is None:
+            copy.wait_send()
+        else:
+            pl.when(there)(copy.wait_send)
 
 
 def solution(mesh):
@@ -426,7 +477,9 @@
                 vmem((3, 3, 8, 128), F32),
                 vmem((2, 2, 512, 512), F32),
                 vmem((2, 2, RIM, 512), F32),
-                vmem((2, 2, RIM, 512), F32),
+                vmem((2, 2, RIM, WIN), F32),
+                vmem((2, 2, RIM, WIN), F32),
+                vmem((2, 2, RIM, RIM), F32),
                 vmem((2, 2, WIN, RIM), F32),
                 vmem((2, 2, WIN, RIM), F32),
                 vmem((2, 2, 2, WIN, RIM), F32),

time: 88 us -> 77.8 us (0.88)
  the two profiles are of different devices: /device:TPU:1 before, /device:TPU:104 now
where the time goes in v2:
time: 77.8 us; the launch traced here: 77.7 us
  Pallas kernels  75.4 us (97%)
  local copies, waits for them, and re-layouts  2.29 us (3%)
    pallas_call x1, Pallas kernels, step(): pl.pallas_call(functools.partial(kernel, rows, cols), name='adjoint', out...  75.4 us
    unnamed x1, local copies, waits for them, and re-layouts  2.29 us

profile of v2, /device:TPU:104, one launch (start us, length us, event | category | flops | bytes accessed | tf_op | source)
XLA Modules:
  0.0 77.7 jit_solution(4763300724715196945)
XLA Ops:
  0.0 75.4 %adjoint.1 = f32[2,2,256,256]{3,2,1,0:T(8,128)} custom-call(s32[2,2]{1,0:T(2,128)} %bitcast.5, f32[2,2,256,256]{3,2,1,0:T(8,128)} %obj_hbm.1, f32[2,256,256]{2,1,0:T(8,128)} %probe_hbm.1, bf16[2,512,256]{2,1,0:T(8,128)(2,1)} %bitcast.3, bf16[2,2,256,256]{3,2,1,0:T(8,128)(2,1)} %bitcast.4, bf16[4,256,256]{2,1,0:T(8,128)(2,1)} %constant.4.clone.tab_hbm, ...), custom_call_target="tpu_custom_call" | custom-call | tf_op jit(solution)/shard_map/adjoint/pallas_call | solution.py:462
  75.4 2.3 %copy.9 = f32[2,2,256,256]{3,2,1,0:T(8,128)} copy(f32[2,2,256,256]{3,2,1,0:T(8,128)} %adjoint.1) | data formatting | bytes 2097152

commit v3 on v2

--- a/solution.py
+++ b/solution.py
@@ -17,12 +17,12 @@
 F32 = jnp.float32
 BF16 = jnp.bfloat16
 
-O_RIGHT, O_LEFT = 0, 1
-C_INNER, C_STRAIGHT, C_DIAGONAL, C_EDGE = 2, 3, 4, 5
-H_INNER, H_STRAIGHT, H_DIAGONAL = 6, 8, 9
-POS_RIGHT, POS_LEFT, POS_INNER, POS_OUTER = 10, 11, 12, 13
-GRAD = 14
-COPIES = GRAD + 12
+O_RIGHT, O_LEFT = 0, 2
+C_INNER, C_STRAIGHT, C_DIAGONAL, C_EDGE = 4, 5, 6, 7
+H_INNER, H_STRAIGHT, H_DIAGONAL = 8, 10, 11
+POS_RIGHT, POS_LEFT, POS_INNER, POS_OUTER = 12, 13, 14, 15
+GRAD = 16
+COPIES = GRAD + 16
 
 
 def split(values):
@@ -54,14 +54,15 @@
 def kernel(
     rows,
     cols,
-    pos_ref,
+    pos_hbm,
     obj_hbm,
     probe_hbm,
     res_hbm,
     sav_hbm,
     tab_hbm,
     atab_hbm,
-    out_hbm,
+    out,
+    pos_ref,
     obj,
     probe,
     res,
@@ -90,7 +91,6 @@
     pbuf,
     lsq,
     light,
-    obuf,
     send_sem,
     recv_sem,
     load_sem,
@@ -123,6 +123,7 @@
         copy.start()
         loads.append(copy)
 
+    load(pos_hbm, pos_ref)
     load(res_hbm, res.at[:, 0:512])
     load(res_hbm, res.at[:, 512:1024])
     load(tab_hbm, tab)
@@ -179,8 +180,14 @@
             else:
                 pl.when(comes)(copy.wait_recv)
 
-    send(obj_hbm.at[1, :, :, RIM:], ext.at[:, RIM : 3 * RIM, 0:RIM], O_RIGHT, right, has_right, has_left)
-    send(obj_hbm.at[1, :, :, 0:RIM], ext.at[:, RIM : 3 * RIM, 3 * RIM :], O_LEFT, left, has_left, has_right)
+    loads[0].wait()
+    for number in range(2):
+        for axis in range(2):
+            value = pos_ref[number, axis].astype(F32)
+            posx[1, 2 * number + axis : 2 * number + axis + 1, :] = jnp.full((1, 128), value, F32)
+    posx[1, 4:8, :] = jnp.zeros((4, 128), F32)
+    send(posx.at[1], posx.at[0], POS_RIGHT, right, has_right, has_left)
+    send(posx.at[1], posx.at[2], POS_LEFT, left, has_left, has_right)
     near = 128 * parity
     halo = 384 * parity
     over = WIN * (1 - 2 * parity)
@@ -188,6 +195,10 @@
     above = RIM - RIM * core
     outside = 3 * RIM * (1 - core)
     inside_row = 3 * RIM * core
+    for part, start in ((0, below), (1, above)):
+        tall = cut(start)
+        send(obj_hbm.at[1, :, tall, RIM:], ext.at[:, cut(RIM + start), 0:RIM], O_RIGHT + part, right, has_right, has_left)
+        send(obj_hbm.at[1, :, tall, 0:RIM], ext.at[:, cut(RIM + start), 3 * RIM :], O_LEFT + part, left, has_left, has_right)
     send(obj_hbm.at[1, :, cut(below), cut(near)], ext.at[:, cut(outside), cut(RIM + near)], C_STRAIGHT, outer, has_outer)
     send(
         obj_hbm.at[1, :, cut(below), cut(near)],
@@ -205,13 +216,6 @@
         lone,
     )
     send(obj_hbm.at[1, :, cut(above), :], ext.at[:, cut(inside_row), RIM : 3 * RIM], C_INNER, inner)
-    for number in range(2):
-        for axis in range(2):
-            value = pos_ref[number, axis].astype(F32)
-            posx[1, 2 * number + axis : 2 * number + axis + 1, :] = jnp.full((1, 128), value, F32)
-    posx[1, 4:8, :] = jnp.zeros((4, 128), F32)
-    send(posx.at[1], posx.at[0], POS_RIGHT, right, has_right, has_left)
-    send(posx.at[1], posx.at[2], POS_LEFT, left, has_left, has_right)
 
     row_index = lax.broadcasted_iota(jnp.int32, (WIN, WIN), 0)
     col_index = lax.broadcasted_iota(jnp.int32, (WIN, WIN), 1)
@@ -234,7 +238,7 @@
                 spot = (slice(a * WIN, (a + 1) * WIN), slice(b * WIN, (b + 1) * WIN))
                 target[spot] = target[spot] + jnp.where(hit, field, 0.0)
 
-    for copy in loads:
+    for copy in loads[1:]:
         copy.wait()
 
     def first(number, carry):
@@ -297,37 +301,41 @@
     lsq[1] = low
 
     def send_rows(group):
-        base = GRAD + 6 * group
+        base = GRAD + 8 * group
         send(frame.at[group, :, cut(3 * RIM * core), cut(WIN - WIN * parity, WIN)], straight.at[group], base + 1, outer, has_outer)
         send(frame.at[group, :, cut(3 * RIM * core), cut(WIN * parity, WIN)], slanted.at[group], base + 2, diagonal, has_diagonal)
         send(frame.at[group, :, cut(3 * RIM * core), cut(RIM + near)], edge.at[group], base + 3, outer, lone, facing)
         send(frame.at[group, :, cut(3 * RIM - 3 * RIM * core), :], within.at[group], base, inner)
 
-    def send_sides(group):
-        base = GRAD + 6 * group
-        arrived(base, base + 1, base + 2, base + 3)
-        for part in range(2):
-            spot = (group, part, cut(WIN - RIM * core), slice(None))
-            frame[spot] = frame[spot] + within[group, part]
-            spot = (group, part, cut(RIM + RIM * core), cut(WIN * parity, WIN))
-            for there, piece in ((has_outer, straight), (has_diagonal, slanted)):
-                @pl.when(there)
+    def send_sides(group, part):
+        base = GRAD + 8 * group
+        start = below if part == 0 else above
+        tall = cut(RIM + start)
+        if part == 1:
+            arrived(base)
+            for plane in range(2):
+                frame[group, plane, tall, :] = frame[group, plane, tall, :] + within[group, plane]
+        else:
+            arrived(base + 1, base + 2, base + 3)
+            for plane in range(2):
+                spot = (group, plane, tall, cut(WIN * parity, WIN))
+                for there, piece in ((has_outer, straight), (has_diagonal, slanted)):
+                    @pl.when(there)
+                    def _():
+                        frame[spot] = frame[spot] + piece[group, plane]
+
+                @pl.when(facing)
                 def _():
-                    frame[spot] = frame[spot] + piece[group, part]
-
-            @pl.when(facing)
-            def _():
-                spot = (group, part, cut(RIM + RIM * core), cut(WIN - near))
-                frame[spot] = frame[spot] + edge[group, part]
-
-        middle = slice(RIM, 3 * RIM)
-        side[group, 0] = frame[group, :, middle, 3 * RIM :]
-        side[group, 1] = frame[group, :, middle, 0:RIM]
-        send(side.at[group, 0], from_left.at[group], base + 4, right, has_right, has_left)
-        send(side.at[group, 1], from_right.at[group], base + 5, left, has_left, has_right)
+                    spot = (group, plane, tall, cut(WIN - near))
+                    frame[spot] = frame[spot] + edge[group, plane]
+
+        side[group, part, 0] = frame[group, :, tall, 3 * RIM :]
+        side[group, part, 1] = frame[group, :, tall, 0:RIM]
+        send(side.at[group, part, 0], from_left.at[group, :, cut(start)], base + 4 + part, right, has_right, has_left)
+        send(side.at[group, part, 1], from_right.at[group, :, cut(start)], base + 6 + part, left, has_left, has_right)
 
     def finish(group):
-        base = GRAD + 6 * group
+        base = GRAD + 8 * group
 
         @pl.when(gx == 0)
         def _():
@@ -337,7 +345,7 @@
         def _():
             from_right[group] = jnp.zeros((2, WIN, RIM), F32)
 
-        arrived(base + 4, base + 5)
+        arrived(base + 4, base + 5, base + 6, base + 7)
         for part in range(2):
             for v, horizontal in ((0, from_left), (1, from_right)):
                 wide = slice(v * RIM, v * RIM + RIM)
@@ -345,25 +353,18 @@
                     frame[group, part, RIM : 3 * RIM, RIM + v * RIM : 2 * RIM + v * RIM]
                     + horizontal[group, part]
                 )
-                obuf[1 - group, part, :, wide] = obj[1 - group, part, :, wide] - total / light[:, wide]
-        copy = pltpu.make_async_copy(obuf.at[1 - group], out_hbm.at[1 - group], load_sem.at[8 + group])
-        copy.start()
-        return copy
-
+                out[1 - group, part, :, wide] = obj[1 - group, part, :, wide] - total / light[:, wide]
+
+    arrived(POS_RIGHT, POS_LEFT)
+    posall[1] = posx[...]
+    send(posx, posall.at[2 * core], POS_INNER, inner)
+    send(posx, posall.at[2 - 2 * core], POS_OUTER, outer, has_outer)
     arrived(O_RIGHT, O_LEFT)
     rows_out, rows_in = cut(RIM + below), cut(RIM + above)
     send(ext.at[:, rows_out, cut(halo)], ext.at[:, cut(outside), cut(halo)], H_STRAIGHT, outer, has_outer)
     send(ext.at[:, rows_out, cut(halo)], ext.at[:, cut(outside), cut(halo + over)], H_DIAGONAL, diagonal, has_diagonal)
-    for v, span in ((0, slice(0, RIM)), (1, slice(3 * RIM, 4 * RIM))):
-        send(ext.at[:, rows_in, span], ext.at[:, cut(inside_row), span], H_INNER + v, inner)
-    arrived(POS_RIGHT, POS_LEFT)
-    posall[1] = posx[...]
-    send(posx, posall.at[2 - 2 * (1 - core)], POS_INNER, inner)
-    send(posx, posall.at[2 - 2 * core], POS_OUTER, outer, has_outer)
     send_rows(0)
 
-    light[...] = jnp.full((WIN, WIN), ridge, F32)
-    arrived(POS_INNER, POS_OUTER)
     offset = (row_index - col_index).astype(F32)
 
     def lit(number, carry):
@@ -385,8 +386,11 @@
         light[...] = total
         return carry
 
-    lax.fori_loop(0, 9, lit, 0)
-
+
+    arrived(O_RIGHT + 1, O_LEFT + 1)
+    for v, span in ((0, slice(0, RIM)), (1, slice(3 * RIM, 4 * RIM))):
+        send(ext.at[:, rows_in, span], ext.at[:, cut(inside_row), span], H_INNER + v, inner)
+    send_sides(0, 1)
     arrived(C_INNER, C_STRAIGHT, C_DIAGONAL, C_EDGE, H_INNER, H_INNER + 1, H_STRAIGHT, H_DIAGONAL)
 
     first_row = jnp.where(gy == 0, RIM, 0)
@@ -439,11 +443,14 @@
 
     lax.fori_loop(0, 2, second, 0)
     send_rows(1)
-    send_sides(0)
-    send_sides(1)
-    stores = [finish(0), finish(1)]
-    for copy in stores:
-        copy.wait()
+    send_sides(0, 0)
+    light[...] = jnp.full((WIN, WIN), ridge, F32)
+    arrived(POS_INNER, POS_OUTER)
+    lax.fori_loop(0, 9, lit, 0)
+    send_sides(1, 1)
+    send_sides(1, 0)
+    finish(0)
+    finish(1)
     for number in range(COPIES):
         copy, there, _ = copies[number]
         if there is None:
@@ -452,20 +459,31 @@
             pl.when(there)(copy.wait_send)
 
 
+def store(result, out_hbm, sem):
+    copies = [
+        pltpu.make_async_copy(result.at[k // 2, k % 2], out_hbm.at[k // 2, k % 2], sem.at[k]) for k in range(4)
+    ]
+    for copy in copies:
+        copy.start()
+    for copy in copies:
+        copy.wait()
+
+
 def solution(mesh):
     rows, cols = mesh.shape["gy"], mesh.shape["gx"]
     tab, atab = constant_tables()
 
     def step(object_field, probe, positions, residual, saved_wave):
-        anywhere = pl.BlockSpec(memory_space=pl.ANY)
+        anywhere = pl.BlockSpec(memory_space=pltpu.HBM)
         vmem = pltpu.VMEM
-        return pl.pallas_call(
+        result = pl.pallas_call(
             functools.partial(kernel, rows, cols),
             name="adjoint",
             out_shape=jax.ShapeDtypeStruct((2, 2, WIN, WIN), F32),
-            in_specs=[pl.BlockSpec(memory_space=pltpu.SMEM)] + [anywhere] * 6,
-            out_specs=anywhere,
+            in_specs=[anywhere] * 7,
+            out_specs=pl.BlockSpec(memory_space=pltpu.VMEM),
             scratch_shapes=[
+                pltpu.SMEM((2, 2), jnp.int32),
                 vmem((2, 2, WIN, WIN), F32),
                 vmem((2, WIN, WIN), F32),
                 vmem((2, 1024, WIN), BF16),
@@ -482,7 +500,7 @@
                 vmem((2, 2, RIM, RIM), F32),
                 vmem((2, 2, WIN, RIM), F32),
                 vmem((2, 2, WIN, RIM), F32),
-                vmem((2, 2, 2, WIN, RIM), F32),
+                vmem((2, 2, 2, 2, RIM, RIM), F32),
                 vmem((512, 1024), BF16),
                 vmem((1536, 512), BF16),
                 vmem((512, 1536), BF16),
@@ -494,23 +512,36 @@
                 vmem((2, 2, WIN, WIN), F32),
                 vmem((2, WIN, WIN), BF16),
                 vmem((WIN, WIN), F32),
-                vmem((2, 2, WIN, WIN), F32),
                 pltpu.SemaphoreType.DMA((COPIES,)),
                 pltpu.SemaphoreType.DMA((COPIES,)),
-                pltpu.SemaphoreType.DMA((10,)),
+                pltpu.SemaphoreType.DMA((9,)),
             ],
             compiler_params=pltpu.CompilerParams(
-                collective_id=0, has_side_effects=True, vmem_limit_bytes=56 * 1024 * 1024
+                collective_id=0, has_side_effects=True, vmem_limit_bytes=40 * 1024 * 1024
             ),
         )(
-            positions.reshape(2, 2),
-            object_field,
-            probe,
-            residual.reshape(2, 512, WIN),
-            saved_wave.reshape(2, 2, WIN, WIN),
-            jnp.asarray(tab),
-            jnp.asarray(atab),
+            *(
+                pltpu.with_memory_space_constraint(x, pltpu.HBM)
+                for x in (
+                    positions.reshape(2, 2),
+                    object_field,
+                    probe,
+                    residual.reshape(2, 512, WIN),
+                    saved_wave.reshape(2, 2, WIN, WIN),
+                    jnp.asarray(tab),
+                    jnp.asarray(atab),
+                )
+            ),
         )
+        return pl.pallas_call(
+            store,
+            name="store",
+            out_shape=jax.ShapeDtypeStruct((2, 2, WIN, WIN), F32),
+            in_specs=[pl.BlockSpec(memory_space=pltpu.VMEM)],
+            out_specs=anywhere,
+            scratch_shapes=[pltpu.SemaphoreType.DMA((4,))],
+            compiler_params=pltpu.CompilerParams(vmem_limit_bytes=2 * 1024 * 1024),
+        )(result)
 
     placed = (
         P(None, None, "gy", "gx"),

time: 77.8 us -> 68.6 us (0.88)
  the two profiles are of different devices: /device:TPU:104 before, /device:TPU:43 now
where the time goes in v3:
time: 68.6 us; the launch traced here: 68.5 us
  Pallas kernels  68.5 us (100%)
    pallas_call x1, Pallas kernels, step(): pl.pallas_call(functools.partial(kernel, rows, cols), name='adjoint', out...  67.5 us

profile of v3, /device:TPU:43, one launch (start us, length us, event | category | flops | bytes accessed | tf_op | source)
XLA Modules:
  0.0 68.5 jit_solution(4108551562474628864)
XLA Ops:
  0.0 67.5 %adjoint.1.result = f32[2,2,256,256]{3,2,1,0:T(8,128)S(1)} custom-call(s32[2,2]{1,0:T(2,128)} %bitcast.5, f32[2,2,256,256]{3,2,1,0:T(8,128)} %obj_hbm.1, f32[2,256,256]{2,1,0:T(8,128)} %probe_hbm.1, bf16[2,512,256]{2,1,0:T(8,128)(2,1)} %bitcast.3, bf16[2,2,256,256]{3,2,1,0:T(8,128)(2,1)} %bitcast.4, bf16[4,256,256]{2,1,0:T(8,128)(2,1)} %constant.4.clone.tab_hbm, ...), custom_call_target="tpu_custom_call" | custom-call | tf_op jit(solution)/shard_map/adjoint/pallas_call | solution.py:479
  67.5 1.0 %store.1 = f32[2,2,256,256]{3,2,1,0:T(8,128)} custom-call(f32[2,2,256,256]{3,2,1,0:T(8,128)S(1)} %adjoint.1.result), custom_call_target="tpu_custom_call" | custom-call | tf_op jit(solution)/shard_map/store/pallas_call | solution.py:536

commit v4 on v3

--- a/solution.py
+++ b/solution.py
@@ -116,6 +116,15 @@
     def cut(start, size=RIM):
         return pl.ds(pl.multiple_of(start, RIM), size)
 
+    barrier = pltpu.get_barrier_semaphore()
+    greeted = 1
+    pl.semaphore_signal(barrier, inc=1, device_id=inner, device_id_type=MESH)
+    for there, who in ((has_left, left), (has_right, right), (has_outer, outer), (has_diagonal, diagonal)):
+        @pl.when(there)
+        def _():
+            pl.semaphore_signal(barrier, inc=1, device_id=who, device_id_type=MESH)
+
+        greeted = greeted + there.astype(jnp.int32)
     loads = []
 
     def load(source, target):
@@ -143,15 +152,6 @@
     def _():
         ext[:, RIM : 3 * RIM, 3 * RIM :] = jnp.zeros((2, WIN, RIM), F32)
 
-    barrier = pltpu.get_barrier_semaphore()
-    greeted = 1
-    pl.semaphore_signal(barrier, inc=1, device_id=inner, device_id_type=MESH)
-    for there, who in ((has_left, left), (has_right, right), (has_outer, outer), (has_diagonal, diagonal)):
-        @pl.when(there)
-        def _():
-            pl.semaphore_signal(barrier, inc=1, device_id=who, device_id_type=MESH)
-
-        greeted = greeted + there.astype(jnp.int32)
     pl.semaphore_wait(barrier, greeted)
 
     copies = {}
@@ -355,27 +355,17 @@
                 )
                 out[1 - group, part, :, wide] = obj[1 - group, part, :, wide] - total / light[:, wide]
 
-    arrived(POS_RIGHT, POS_LEFT)
-    posall[1] = posx[...]
-    send(posx, posall.at[2 * core], POS_INNER, inner)
-    send(posx, posall.at[2 - 2 * core], POS_OUTER, outer, has_outer)
-    arrived(O_RIGHT, O_LEFT)
-    rows_out, rows_in = cut(RIM + below), cut(RIM + above)
-    send(ext.at[:, rows_out, cut(halo)], ext.at[:, cut(outside), cut(halo)], H_STRAIGHT, outer, has_outer)
-    send(ext.at[:, rows_out, cut(halo)], ext.at[:, cut(outside), cut(halo + over)], H_DIAGONAL, diagonal, has_diagonal)
-    send_rows(0)
-
     offset = (row_index - col_index).astype(F32)
 
-    def lit(number, carry):
-        dy = number // 3 - 1
-        dx = number % 3 - 1
+    def lit(line, dx_index, carry):
+        dy = line - 1
+        dx = dx_index - 1
         inside = (gy + dy >= 0) & (gy + dy < rows) & (gx + dx >= 0) & (gx + dx < cols)
         weight = jnp.where(inside, 1.0, 0.0)
-        spots = posall[number // 3, number % 3]
+        spots = posall[line, dx_index]
         total = light[...]
         for spot in range(2):
-            row = spots[2 * spot : 2 * spot + 1, :] + (dy * WIN - RIM).astype(F32)
+            row = spots[2 * spot : 2 * spot + 1, :] + jnp.asarray(dy * WIN - RIM, jnp.int32).astype(F32)
             col = spots[2 * spot + 1 : 2 * spot + 2, :] + (dx * WIN - RIM).astype(F32)
             row = jnp.concatenate([row, row], axis=1)
             col = jnp.concatenate([col, col], axis=1)
@@ -385,6 +375,21 @@
                 total = total + dot(by_rows, dot(lsq[part], by_cols).astype(BF16))
         light[...] = total
         return carry
+
+    def light_of(line):
+        lax.fori_loop(0, 3, functools.partial(lit, line), 0)
+
+    arrived(POS_RIGHT, POS_LEFT)
+    posall[1] = posx[...]
+    send(posx, posall.at[2 * core], POS_INNER, inner)
+    send(posx, posall.at[2 - 2 * core], POS_OUTER, outer, has_outer)
+    light[...] = jnp.full((WIN, WIN), ridge, F32)
+    light_of(1)
+    arrived(O_RIGHT, O_LEFT)
+    rows_out, rows_in = cut(RIM + below), cut(RIM + above)
+    send(ext.at[:, rows_out, cut(halo)], ext.at[:, cut(outside), cut(halo)], H_STRAIGHT, outer, has_outer)
+    send(ext.at[:, rows_out, cut(halo)], ext.at[:, cut(outside), cut(halo + over)], H_DIAGONAL, diagonal, has_diagonal)
+    send_rows(0)
 
 
     arrived(O_RIGHT + 1, O_LEFT + 1)
@@ -443,12 +448,13 @@
 
     lax.fori_loop(0, 2, second, 0)
     send_rows(1)
+    send_sides(1, 1)
     send_sides(0, 0)
-    light[...] = jnp.full((WIN, WIN), ridge, F32)
-    arrived(POS_INNER, POS_OUTER)
-    lax.fori_loop(0, 9, lit, 0)
-    send_sides(1, 1)
+    arrived(POS_INNER)
+    light_of(2 - 2 * core)
     send_sides(1, 0)
+    arrived(POS_OUTER)
+    light_of(2 * core)
     finish(0)
     finish(1)
     for number in range(COPIES):

time: 68.6 us -> 68.2 us (level)
  no operation moved by 1% of the time
where the time goes in v4:
time: 68.2 us; the launch traced here: 68.1 us
  Pallas kernels  68.1 us (100%)
    pallas_call x1, Pallas kernels, step(): pl.pallas_call(functools.partial(kernel, rows, cols), name='adjoint', out...  67.1 us

profile of v4, /device:TPU:43, one launch (start us, length us, event | category | flops | bytes accessed | tf_op | source)
XLA Modules:
  0.0 68.1 jit_solution(9017434400095132659)
XLA Ops:
  0.0 67.1 %adjoint.1.result = f32[2,2,256,256]{3,2,1,0:T(8,128)S(1)} custom-call(s32[2,2]{1,0:T(2,128)} %bitcast.5, f32[2,2,256,256]{3,2,1,0:T(8,128)} %obj_hbm.1, f32[2,256,256]{2,1,0:T(8,128)} %probe_hbm.1, bf16[2,512,256]{2,1,0:T(8,128)(2,1)} %bitcast.3, bf16[2,2,256,256]{3,2,1,0:T(8,128)(2,1)} %bitcast.4, bf16[4,256,256]{2,1,0:T(8,128)(2,1)} %constant.4.clone.tab_hbm, ...), custom_call_target="tpu_custom_call" | custom-call | tf_op jit(solution)/shard_map/adjoint/pallas_call | solution.py:485
  67.1 1.0 %store.1 = f32[2,2,256,256]{3,2,1,0:T(8,128)} custom-call(f32[2,2,256,256]{3,2,1,0:T(8,128)S(1)} %adjoint.1.result), custom_call_target="tpu_custom_call" | custom-call | tf_op jit(solution)/shard_map/store/pallas_call | solution.py:542
